TPU v7x, 256 devices: a whole 4x4x8 slice. The times are simulated.
256 devices in a mesh: tile: 64 (over y, z_hi, x), mode: 4 (over z_lo, core).
Axes of the slice: x: 4, y: 4, z: 8 (z_hi: 4, z_lo: 2; z = z_hi * 2 + z_lo), core: 2. Of those that a mesh axis runs over, the one named last changes fastest.
Arguments:
- object_tiles: float32 [64, 2, 2, 128, 128], P('tile'), may hold values from -1.5 to 1.5
- probe: float32 [16, 2, 128, 128], P('mode'), may hold values from -1 to 1
- propagator_phase: float32 [128, 128], replicated, may hold values from -3.140625 to 3.140625
- measured: float32 [256, 128, 128], P('tile'), may hold values from 0.25 to 2
- positions: int32 [256, 2], P('tile'), may hold values from 0 to 128, as said below
Outputs:
- updated_object: float32 [64, 2, 2, 128, 128], P('tile')
- intensity: float32 [256, 128, 128], P('tile')
Inputs may be any that keep to these rules, and one draw needn't show every extreme that they name: `positions`: row and column of the top-left cell of a pattern's 128 x 128 window within its tile's extended region.
All inputs are finite; a program needn't handle non-finite values.
Results may differ from a plain program's by a relative error of at most 0.0003.
Values sent between devices are 32-bit elements; how exact they have to be, the bound alone decides.
A program may use at most 64 MiB of HBM per device.

v0:
```python
import math

import jax
import jax.numpy as jnp
from jax import lax
from jax.sharding import PartitionSpec as P

K = 128
HALO = 64
STEPS = 2
TILE_COLS = 8


learning_rate = 0.5


def with_halo(block, sides, width):
    for axis, dim in sides:
        count = lax.axis_size(axis)
        forward = [(i, i + 1) for i in range(count - 1)]
        forward.append((count - 1, 0))
        backward = [(target, source) for source, target in forward]
        low = lax.ppermute(
            lax.slice_in_dim(block, block.shape[dim] - width, None, axis=dim), axis, forward
        )
        high = lax.ppermute(lax.slice_in_dim(block, 0, width, axis=dim), axis, backward)
        block = jnp.concatenate([low, block, high], axis=dim)
    return block


def from_behind(value, axis, steps):
    count = lax.axis_size(axis)
    first, last = (max(0, -steps), min(count, count - steps))
    return lax.ppermute(value, axis, [(source, source + steps) for source in range(first, last)])


def over_pieces(value, axis):
    return lax.all_gather(value, axis).sum(0)


def in_blocks(value, dim, length):
    lengths = value.shape
    tiles = value.reshape(*lengths[:dim], length, lengths[dim] // length, *lengths[dim + 1 :])
    return jnp.moveaxis(tiles, dim, 0)


def sent_and_summed(value, axis, dim):
    length = lax.axis_size(axis)
    tiles = lax.all_to_all(in_blocks(value, dim, length), axis, 0, 0, tiled=True)
    return jnp.sum(tiles, axis=0)


def laid_out(tiles, dim):
    tiles = jnp.moveaxis(tiles, 0, dim)
    lengths = tiles.shape
    return tiles.reshape(*lengths[:dim], lengths[dim] * lengths[dim + 1], *lengths[dim + 2 :])


def sent_to_all(value, axis):
    copies = jnp.broadcast_to(value, (lax.axis_size(axis), *value.shape))
    return lax.all_to_all(copies, axis, split_axis=0, concat_axis=0, tiled=True)


def collect(value, axis, dim):
    return laid_out(sent_to_all(value, axis), dim)


def dft_tables(order_size):
    index = jnp.arange(order_size, dtype=jnp.int32)
    product = index[:, None] * index[None, :] % order_size
    angle = product.astype(jnp.float32) * (2.0 * math.pi / order_size)
    factor = 1.0 / math.sqrt(order_size)
    return (jnp.cos(angle) * factor, -jnp.sin(angle) * factor)


def product_left(matrix, operand):
    return jnp.einsum("jk,...kl->...jl", matrix, operand, precision=lax.Precision.HIGHEST)


def product_right(operand, matrix):
    return jnp.einsum("...jk,kl->...jl", operand, matrix, precision=lax.Precision.HIGHEST)


def transform(real_part, imag_part, cos_table, sin_table):
    left_real = product_left(cos_table, real_part) - product_left(sin_table, imag_part)
    left_imag = product_left(cos_table, imag_part) + product_left(sin_table, real_part)
    out_real = product_right(left_real, cos_table) - product_right(left_imag, sin_table)
    out_imag = product_right(left_imag, cos_table) + product_right(left_real, sin_table)
    return (out_real, out_imag)


def multislice(windows, probe, propagator_phase):
    order_size = probe.shape[-1]
    cos_table, sin_table = dft_tables(order_size)
    kernel_cos = jnp.cos(propagator_phase)
    kernel_sin = jnp.sin(propagator_phase)
    wave_real = probe[None, :, 0]
    wave_imag = probe[None, :, 1]
    layers = windows.shape[1]
    for layer_index in range(layers):
        trans_real = 1.0 + windows[:, None, layer_index, 0]
        trans_imag = windows[:, None, layer_index, 1]
        wave_real, wave_imag = (
            trans_real * wave_real - trans_imag * wave_imag,
            trans_real * wave_imag + trans_imag * wave_real,
        )
        if layer_index + 1 < layers:
            spec_real, spec_imag = transform(wave_real, wave_imag, cos_table, sin_table)
            spec_real, spec_imag = (
                kernel_cos * spec_real - kernel_sin * spec_imag,
                kernel_cos * spec_imag + kernel_sin * spec_real,
            )
            wave_real, wave_imag = transform(spec_real, spec_imag, cos_table, -sin_table)
    return transform(wave_real, wave_imag, cos_table, sin_table)


def windows_of(extended, positions, order_size):
    anchor = jnp.zeros((), jnp.int32)

    def single_window(position):
        starts = (anchor, anchor, position[0], position[1])
        return lax.dynamic_slice(extended, starts, (extended.shape[0], 2, order_size, order_size))

    return jax.vmap(single_window)(positions)


def grow_columns(planes):
    return with_halo(planes, (("tile", 2),), HALO)


def grow_rows(planes):
    last = planes.shape[1]
    from_top = from_behind(planes[:, last - HALO :, :], "tile", TILE_COLS)
    from_bottom = from_behind(planes[:, :HALO, :], "tile", -TILE_COLS)
    return jnp.concatenate([from_top, planes, from_bottom], axis=1)


def fetch(planes):
    return grow_rows(grow_columns(planes))


def fold(planes):
    core_size = planes.shape[1] - 2 * HALO
    taller = grow_rows(planes)
    middle = taller[:, 2 * HALO : 2 * HALO + core_size]
    middle = middle.at[:, :HALO].add(taller[:, :HALO])
    middle = middle.at[:, core_size - HALO :].add(taller[:, taller.shape[1] - HALO :])
    widened = grow_columns(middle)
    result = widened[:, :, 2 * HALO : 2 * HALO + core_size]
    result = result.at[:, :, :HALO].add(widened[:, :, :HALO])
    return result.at[:, :, core_size - HALO :].add(widened[:, :, widened.shape[2] - HALO :])


def local(object_tiles, probe, propagator_phase, measured, positions):
    layers = object_tiles.shape[1]
    core_size = object_tiles.shape[3]
    extent = core_size + 2 * HALO
    planes = object_tiles.reshape(layers * 2, core_size, core_size)
    extended = fetch(planes)
    per_step = positions.shape[0] // STEPS
    results = []
    for iteration in range(STEPS):
        first_row = iteration * per_step
        these_positions = positions[first_row : first_row + per_step]
        these_measured = measured[first_row : first_row + per_step]

        def forward_tile(ext_arg):
            shaped = ext_arg.reshape(layers, 2, extent, extent)
            return multislice(windows_of(shaped, these_positions, K), probe, propagator_phase)

        (spec_real, spec_imag), pullback = jax.vjp(forward_tile, extended)
        partial_sum = jnp.sum(spec_real * spec_real + spec_imag * spec_imag, axis=1)
        intensity = over_pieces(partial_sum, "mode")
        residual = intensity - these_measured
        (gradient,) = pullback(
            (2.0 * residual[:, None] * spec_real, 2.0 * residual[:, None] * spec_imag)
        )
        results.append(intensity)
        gradient_part = sent_and_summed(gradient, "mode", 0)
        share_rows = gradient_part.shape[0]
        own_share = lax.dynamic_slice_in_dim(
            planes, lax.axis_index("mode") * share_rows, share_rows, 0
        )
        own_share = own_share - learning_rate * fold(gradient_part)
        grown = fetch(own_share)
        extended = collect(grown, "mode", 0)
        planes = extended[:, HALO : HALO + core_size, HALO : HALO + core_size]
    updated = planes.reshape(1, layers, 2, core_size, core_size)
    return (updated, jnp.concatenate(results, axis=0))


def solution(mesh):
    return jax.shard_map(
        local,
        mesh=mesh,
        in_specs=(
            P("tile", None, None, None, None),
            P("mode", None, None, None),
            P(),
            P("tile", None, None),
            P("tile", None),
        ),
        out_specs=(P("tile", None, None, None, None), P("tile", None, None)),
        check_vma=False,
    )
```

profile of v0, /device:TPU:78, one launch (start us, length us, event | category | flops | bytes accessed | tf_op | source)
XLA Modules:
  0.0 410.2 jit_solution(133611443076439331)
XLA Ops:
  1.9 4.5 %collective-permute-start = (f32[4,128,64]{2,1,0:T(8,128)S(1)}, f32[4,128,64]{2,1,0:T(8,128)S(1)}, u32[]{:S(2)}, u32[]{:S(2)}) collective-permute-start(f32[4,128,64]{2,1,0:T(8,128)S(1)} %get-tuple-element.230), channel_id=1, source_target_pairs={{0,4},{4,8},{8,12},{12,16},{16,20},{20,24},{24,28},{28,32},{32,36}... | collective-permute-start | bytes 393224 | tf_op jit(solution)/shard_map/ppermute | solution.py:23
  7.5 9.9 %collective-permute-done = f32[4,128,64]{2,1,0:T(8,128)S(1)} collective-permute-done((f32[4,128,64]{2,1,0:T(8,128)S(1)}, f32[4,128,64]{2,1,0:T(8,128)S(1)}, u32[]{:S(2)}, u32[]{:S(2)}) %collective-permute-start) | collective-permute-done | bytes 131104 | tf_op jit(solution)/shard_map/ppermute | solution.py:23
  17.4 6.4 %collective-permute-done.1 = f32[4,128,64]{2,1,0:T(8,128)S(1)} collective-permute-done((f32[4,128,64]{2,1,0:T(8,128)S(1)}, f32[4,128,64]{2,1,0:T(8,128)S(1)}, u32[]{:S(2)}, u32[]{:S(2)}) %collective-permute-start.1) | collective-permute-done | bytes 131104 | tf_op jit(solution)/shard_map/ppermute | solution.py:26
  24.2 4.3 %collective-permute-start.2 = (f32[4,64,256]{2,1,0:T(8,128)S(1)}, f32[4,64,256]{2,1,0:T(8,128)S(1)}, u32[]{:S(2)}, u32[]{:S(2)}) collective-permute-start(f32[4,64,256]{2,1,0:T(8,128)S(1)} %get-tuple-element.224), channel_id=1, source_target_pairs={{0,32},{4,36},{8,40},{12,44},{16,48},{20,52},{24,56},{28,60},{32,6... | collective-permute-start | bytes 786440 | tf_op jit(solution)/shard_map/ppermute | solution.py:34
  28.4 6.4 %collective-permute-start.3 = (f32[4,64,256]{2,1,0:T(8,128)S(1)}, f32[4,64,256]{2,1,0:T(8,128)S(1)}, u32[]{:S(2)}, u32[]{:S(2)}) collective-permute-start(f32[4,64,256]{2,1,0:T(8,128)S(1)} %get-tuple-element.225), channel_id=1, source_target_pairs={{32,0},{36,4},{40,8},{44,12},{48,16},{52,20},{56,24},{60,28},{64,3... | collective-permute-start | bytes 786440 | tf_op jit(solution)/shard_map/ppermute | solution.py:34
  36.8 7.9 %collective-permute-done.2 = f32[4,64,256]{2,1,0:T(8,128)S(1)} collective-permute-done((f32[4,64,256]{2,1,0:T(8,128)S(1)}, f32[4,64,256]{2,1,0:T(8,128)S(1)}, u32[]{:S(2)}, u32[]{:S(2)}) %collective-permute-start.2) | collective-permute-done | bytes 262176 | tf_op jit(solution)/shard_map/ppermute | solution.py:34
  44.7 6.9 %collective-permute-done.3 = f32[4,64,256]{2,1,0:T(8,128)S(1)} collective-permute-done((f32[4,64,256]{2,1,0:T(8,128)S(1)}, f32[4,64,256]{2,1,0:T(8,128)S(1)}, u32[]{:S(2)}, u32[]{:S(2)}) %collective-permute-start.3) | collective-permute-done | bytes 262176 | tf_op jit(solution)/shard_map/ppermute | solution.py:34
  51.8 4.4 %while.12 = (s32[]{:T(128)}, f32[2,2,256,256]{3,2,1,0:T(8,128)S(1)}, s32[2,4]{1,0:T(2,128)S(1)}, f32[2,2,2,128,128]{4,3,2,1,0:T(8,128)S(1)}, s32[]{:T(128)}) while((s32[]{:T(128)}, f32[2,2,256,256]{3,2,1,0:T(8,128)S(1)}, s32[2,4]{1,0:T(2,128)S(1)}, f32[2,2,2,128,128]{4,3,2,1,0:T(8,128)S(1)}, s32[]{:T(128)}) %tuple.163), condition=%wide.while_cond.8, body=%wide.while_body.8.sunk | while | flops 2 | bytes 524421 | solution.py:122
  83.7 7.4 %all-gather = f32[8,128,128]{2,1,0:T(8,128)} all-gather(f32[2,128,128]{2,1,0:T(8,128)S(1)} %get-tuple-element.252), channel_id=2, replica_groups=mesh['tile'=64,'mode'=4] {'mode'}, dimensions={0}, use_global_device_ids=true | all-gather | bytes 655360 | tf_op jit(solution)/shard_map/all_gather | solution.py:38
  116.0 19.3 %while.14 = (s32[]{:T(128)}, f32[2,2,256,256]{3,2,1,0:T(8,128)S(1)}, s32[2,4]{1,0:T(2,128)S(1)}, f32[2,2,2,128,128]{4,3,0,2,1:T(8,128)S(1)}, s32[]{:T(128)}, /*index=5*/s32[4]{0:T(128)S(1)}, s32[]{:T(128)}) while((s32[]{:T(128)}, f32[2,2,256,256]{3,2,1,0:T(8,128)S(1)}, s32[2,4]{1,0:T(2,128)S(1)}, f32[2,2,2,128,128]{4,3,0,2,1:T(8,128)S(1)}, ...), condition=%wide.while_cond.10, body=%wide.while_body.10.sunk | while | flops 131101 | bytes 1310923 | solution.py:122
  130.9 4.4 %dynamic-update-slice.40 = f32[2,2,256,256]{3,2,1,0:T(8,128)S(1)} dynamic-update-slice(f32[2,2,256,256]{3,2,1,0:T(8,128)S(1)} %get-tuple-element.409, f32[2,2,128,128]{3,2,1,0:T(8,128)S(1)} %add_select_fusion.5, s32[]{:T(128)} %constant.217.clone.1..sunk, s32[]{:T(128)} %constant.217.clone.1..sunk, s32[]{:T(128)} %bitcast.434, s32[]{:T(128)} %bitcast.435) | dynamic-update-slice | bytes 524292 | tf_op jit(solution)/shard_map/transpose(jvp(vmap()))/scatter-add
  135.3 16.9 %all_to_all.20 = f32[4,1,256,256]{3,2,1,0:T(8,128)S(1)} all-to-all(f32[4,1,256,256]{3,2,1,0:T(8,128)S(1)} %bitcast.447), channel_id=1, replica_groups=mesh['tile'=64,'mode'=4] {'mode'}, dimensions={0} | all-to-all | bytes 2097152 | tf_op jit(solution)/shard_map/all_to_all | solution.py:49
  152.2 12.4 %collective-permute-start.4 = (f32[1,64,256]{2,1,0:T(8,128)S(1)}, f32[1,64,256]{2,1,0:T(8,128)S(1)}, u32[]{:S(2)}, u32[]{:S(2)}) collective-permute-start(f32[1,64,256]{2,1,0:T(8,128)S(1)} %get-tuple-element.229), channel_id=1, source_target_pairs={{0,32},{4,36},{8,40},{12,44},{16,48},{20,52},{24,56},{28,60},{32,6... | collective-permute-start | bytes 196616 | tf_op jit(solution)/shard_map/ppermute | solution.py:34
  167.4 7.4 %collective-permute-done.5 = f32[1,64,256]{2,1,0:T(8,128)S(1)} collective-permute-done((f32[1,64,256]{2,1,0:T(8,128)S(1)}, f32[1,64,256]{2,1,0:T(8,128)S(1)}, u32[]{:S(2)}, u32[]{:S(2)}) %collective-permute-start.5) | collective-permute-done | bytes 65568 | tf_op jit(solution)/shard_map/ppermute | solution.py:34
  179.7 3.9 collective-permute-done.7
  188.7 5.6 %collective-permute-done.9 = f32[1,128,64]{2,1,0:T(8,128)S(1)} collective-permute-done((f32[1,128,64]{2,1,0:T(8,128)S(1)}, f32[1,128,64]{2,1,0:T(8,128)S(1)}, u32[]{:S(2)}, u32[]{:S(2)}) %collective-permute-start.9) | collective-permute-done | bytes 32800 | tf_op jit(solution)/shard_map/ppermute | solution.py:26
  194.4 4.0 collective-permute-start.10
  198.4 6.7 %collective-permute-start.11 = (f32[1,64,256]{2,1,0:T(8,128)S(1)}, f32[1,64,256]{2,1,0:T(8,128)S(1)}, u32[]{:S(2)}, u32[]{:S(2)}) collective-permute-start(f32[1,64,256]{2,1,0:T(8,128)S(1)} %get-tuple-element.237), channel_id=1, source_target_pairs={{32,0},{36,4},{40,8},{44,12},{48,16},{52,20},{56,24},{60,28},{64,3... | collective-permute-start | bytes 196616 | tf_op jit(solution)/shard_map/ppermute | solution.py:34
  213.2 14.4 %all-to-all-done.1 = f32[4,1,256,256]{3,2,1,0:T(8,128)S(1)} async-done(((f32[4,1,256,256]{3,2,1,0:T(8,128)}), f32[4,1,256,256]{3,2,1,0:T(8,128)S(1)}, u32[]{:S(2)}, u32[]{:S(2)}) %all-to-all-start.1) | async-done | bytes 1048608 | tf_op jit(solution)/shard_map/all_to_all | solution.py:61
  227.6 4.4 %while.13 = (s32[]{:T(128)}, f32[2,2,256,256]{3,2,1,0:T(8,128)S(1)}, s32[2,4]{1,0:T(2,128)S(1)}, f32[2,2,2,128,128]{4,3,2,1,0:T(8,128)S(1)}, s32[]{:T(128)}) while((s32[]{:T(128)}, f32[2,2,256,256]{3,2,1,0:T(8,128)S(1)}, s32[2,4]{1,0:T(2,128)S(1)}, f32[2,2,2,128,128]{4,3,2,1,0:T(8,128)S(1)}, s32[]{:T(128)}) %tuple.162), condition=%wide.while_cond.9, body=%wide.while_body.9.sunk | while | flops 2 | bytes 524421 | solution.py:122
  260.3 6.9 %all-gather.1 = f32[8,128,128]{2,1,0:T(8,128)} all-gather(f32[2,128,128]{2,1,0:T(8,128)S(1)} %get-tuple-element.255), channel_id=3, replica_groups=mesh['tile'=64,'mode'=4] {'mode'}, dimensions={0}, use_global_device_ids=true | all-gather | bytes 655360 | tf_op jit(solution)/shard_map/all_gather | solution.py:38
  293.6 20.8 %while.15 = (s32[]{:T(128)}, f32[2,2,256,256]{3,2,1,0:T(8,128)S(1)}, s32[2,4]{1,0:T(2,128)S(1)}, f32[2,2,2,128,128]{4,3,0,2,1:T(8,128)S(1)}, s32[]{:T(128)}, /*index=5*/s32[4]{0:T(128)S(1)}, s32[]{:T(128)}) while((s32[]{:T(128)}, f32[2,2,256,256]{3,2,1,0:T(8,128)S(1)}, s32[2,4]{1,0:T(2,128)S(1)}, f32[2,2,2,128,128]{4,3,0,2,1:T(8,128)S(1)}, ...), condition=%wide.while_cond.11, body=%wide.while_body.11.sunk | while | flops 131101 | bytes 1310923 | solution.py:122
  299.6 4.4 %dynamic-update-slice.41 = f32[2,2,256,256]{3,2,1,0:T(8,128)S(1)} dynamic-update-slice(f32[2,2,256,256]{3,2,1,0:T(8,128)S(1)} %get-tuple-element.445, f32[2,2,128,128]{3,2,1,0:T(8,128)S(1)} %add_select_fusion.6, s32[]{:T(128)} %constant.217.clone.1..sunk.1, s32[]{:T(128)} %constant.217.clone.1..sunk.1, s32[]{:T(128)} %bitcast.441, s32[]{:T(128)} %bitcast.442) | dynamic-update-slice | bytes 524292 | tf_op jit(solution)/shard_map/transpose(jvp(vmap()))/scatter-add
  310.0 4.5 %dynamic-update-slice.41 = f32[2,2,256,256]{3,2,1,0:T(8,128)S(1)} dynamic-update-slice(f32[2,2,256,256]{3,2,1,0:T(8,128)S(1)} %get-tuple-element.445, f32[2,2,128,128]{3,2,1,0:T(8,128)S(1)} %add_select_fusion.6, s32[]{:T(128)} %constant.217.clone.1..sunk.1, s32[]{:T(128)} %constant.217.clone.1..sunk.1, s32[]{:T(128)} %bitcast.441, s32[]{:T(128)} %bitcast.442) | dynamic-update-slice | bytes 524292 | tf_op jit(solution)/shard_map/transpose(jvp(vmap()))/scatter-add
  314.5 17.6 %all_to_all.21 = f32[4,1,256,256]{3,2,1,0:T(8,128)} all-to-all(f32[4,1,256,256]{3,2,1,0:T(8,128)S(1)} %bitcast.448), channel_id=1, replica_groups=mesh['tile'=64,'mode'=4] {'mode'}, dimensions={0} | all-to-all | bytes 2097152 | tf_op jit(solution)/shard_map/all_to_all | solution.py:49
  333.4 8.0 %collective-permute-start.12 = (f32[1,64,256]{2,1,0:T(8,128)S(1)}, f32[1,64,256]{2,1,0:T(8,128)S(1)}, u32[]{:S(2)}, u32[]{:S(2)}) collective-permute-start(f32[1,64,256]{2,1,0:T(8,128)S(1)} %get-tuple-element.227), channel_id=1, source_target_pairs={{0,32},{4,36},{8,40},{12,44},{16,48},{20,52},{24,56},{28,60},{32,6... | collective-permute-start | bytes 196616 | tf_op jit(solution)/shard_map/ppermute | solution.py:34
  344.8 6.8 %collective-permute-done.13 = f32[1,64,256]{2,1,0:T(8,128)S(1)} collective-permute-done((f32[1,64,256]{2,1,0:T(8,128)S(1)}, f32[1,64,256]{2,1,0:T(8,128)S(1)}, u32[]{:S(2)}, u32[]{:S(2)}) %collective-permute-start.13) | collective-permute-done | bytes 65568 | tf_op jit(solution)/shard_map/ppermute | solution.py:34
  356.4 5.3 %collective-permute-done.15 = f32[1,128,64]{2,1,0:T(8,128)S(1)} collective-permute-done((f32[1,128,64]{2,1,0:T(8,128)S(1)}, f32[1,128,64]{2,1,0:T(8,128)S(1)}, u32[]{:S(2)}, u32[]{:S(2)}) %collective-permute-start.15) | collective-permute-done | bytes 32800 | tf_op jit(solution)/shard_map/ppermute | solution.py:26
  366.9 5.1 %collective-permute-done.17 = f32[1,128,64]{2,1,0:T(8,128)S(1)} collective-permute-done((f32[1,128,64]{2,1,0:T(8,128)S(1)}, f32[1,128,64]{2,1,0:T(8,128)S(1)}, u32[]{:S(2)}, u32[]{:S(2)}) %collective-permute-start.17) | collective-permute-done | bytes 32800 | tf_op jit(solution)/shard_map/ppermute | solution.py:26
  372.1 7.5 %collective-permute-start.18 = (f32[1,64,256]{2,1,0:T(8,128)S(1)}, f32[1,64,256]{2,1,0:T(8,128)S(1)}, u32[]{:S(2)}, u32[]{:S(2)}) collective-permute-start(f32[1,64,256]{2,1,0:T(8,128)S(1)} %get-tuple-element.232), channel_id=1, source_target_pairs={{0,32},{4,36},{8,40},{12,44},{16,48},{20,52},{24,56},{28,60},{32,6... | collective-permute-start | bytes 196616 | tf_op jit(solution)/shard_map/ppermute | solution.py:34
  383.1 6.8 %collective-permute-done.19 = f32[1,64,256]{2,1,0:T(8,128)S(1)} collective-permute-done((f32[1,64,256]{2,1,0:T(8,128)S(1)}, f32[1,64,256]{2,1,0:T(8,128)S(1)}, u32[]{:S(2)}, u32[]{:S(2)}) %collective-permute-start.19) | collective-permute-done | bytes 65568 | tf_op jit(solution)/shard_map/ppermute | solution.py:34
  395.4 13.7 %all-to-all-done.3 = f32[4,1,256,256]{3,2,1,0:T(8,128)S(1)} async-done(((f32[4,1,256,256]{3,2,1,0:T(8,128)}), f32[4,1,256,256]{3,2,1,0:T(8,128)S(1)}, u32[]{:S(2)}, u32[]{:S(2)}) %all-to-all-start.3) | async-done | bytes 1048608 | tf_op jit(solution)/shard_map/all_to_all | solution.py:61
  (253 shorter events, 191.7 us)
Async XLA Ops:
  0.6 6.8 %copy-start.5 = (f32[4,2,128,128]{3,2,1,0:T(8,128)S(1)}, f32[4,2,128,128]{3,2,1,0:T(8,128)}, u32[]{:S(2)}) copy-start(f32[4,2,128,128]{3,2,1,0:T(8,128)} %param.22) | copy-start | bytes 1572868
  1.9 15.6 %collective-permute-start = (f32[4,128,64]{2,1,0:T(8,128)S(1)}, f32[4,128,64]{2,1,0:T(8,128)S(1)}, u32[]{:S(2)}, u32[]{:S(2)}) collective-permute-start(f32[4,128,64]{2,1,0:T(8,128)S(1)} %get-tuple-element.230), channel_id=1, source_target_pairs={{0,4},{4,8},{8,12},{12,16},{16,20},{20,24},{24,28},{28,32},{32,36}... | collective-permute-start | bytes 393224 | tf_op jit(solution)/shard_map/ppermute | solution.py:23
  6.3 17.5 %collective-permute-start.1 = (f32[4,128,64]{2,1,0:T(8,128)S(1)}, f32[4,128,64]{2,1,0:T(8,128)S(1)}, u32[]{:S(2)}, u32[]{:S(2)}) collective-permute-start(f32[4,128,64]{2,1,0:T(8,128)S(1)} %get-tuple-element.231), channel_id=1, source_target_pairs={{4,0},{8,4},{12,8},{16,12},{20,16},{24,20},{28,24},{32,28},{36,32}... | collective-permute-start | bytes 393224 | tf_op jit(solution)/shard_map/ppermute | solution.py:26
  6.3 0.7 copy-start.8
  7.5 16.4 %copy-start = (f32[1,2,2,128,128]{4,3,2,1,0:T(8,128)S(1)}, f32[1,2,2,128,128]{4,3,2,1,0:T(8,128)}, u32[]{:S(2)}) copy-start(f32[1,2,2,128,128]{4,3,2,1,0:T(8,128)} %param.21) | copy-start | bytes 786436
  24.2 20.5 %collective-permute-start.2 = (f32[4,64,256]{2,1,0:T(8,128)S(1)}, f32[4,64,256]{2,1,0:T(8,128)S(1)}, u32[]{:S(2)}, u32[]{:S(2)}) collective-permute-start(f32[4,64,256]{2,1,0:T(8,128)S(1)} %get-tuple-element.224), channel_id=1, source_target_pairs={{0,32},{4,36},{8,40},{12,44},{16,48},{20,52},{24,56},{28,60},{32,6... | collective-permute-start | bytes 786440 | tf_op jit(solution)/shard_map/ppermute | solution.py:34
  28.4 23.1 %collective-permute-start.3 = (f32[4,64,256]{2,1,0:T(8,128)S(1)}, f32[4,64,256]{2,1,0:T(8,128)S(1)}, u32[]{:S(2)}, u32[]{:S(2)}) collective-permute-start(f32[4,64,256]{2,1,0:T(8,128)S(1)} %get-tuple-element.225), channel_id=1, source_target_pairs={{32,0},{36,4},{40,8},{44,12},{48,16},{52,20},{56,24},{60,28},{64,3... | collective-permute-start | bytes 786440 | tf_op jit(solution)/shard_map/ppermute | solution.py:34
  34.8 0.7 copy-start.7
  35.7 0.8 copy-start.6
  92.2 1.0 copy-start.2
  152.2 15.2 %collective-permute-start.4 = (f32[1,64,256]{2,1,0:T(8,128)S(1)}, f32[1,64,256]{2,1,0:T(8,128)S(1)}, u32[]{:S(2)}, u32[]{:S(2)}) collective-permute-start(f32[1,64,256]{2,1,0:T(8,128)S(1)} %get-tuple-element.229), channel_id=1, source_target_pairs={{0,32},{4,36},{8,40},{12,44},{16,48},{20,52},{24,56},{28,60},{32,6... | collective-permute-start | bytes 196616 | tf_op jit(solution)/shard_map/ppermute | solution.py:34
  164.6 10.1 %collective-permute-start.5 = (f32[1,64,256]{2,1,0:T(8,128)S(1)}, f32[1,64,256]{2,1,0:T(8,128)S(1)}, u32[]{:S(2)}, u32[]{:S(2)}) collective-permute-start(f32[1,64,256]{2,1,0:T(8,128)S(1)} %get-tuple-element.228), channel_id=1, source_target_pairs={{32,0},{36,4},{40,8},{44,12},{48,16},{52,20},{56,24},{60,28},{64,3... | collective-permute-start | bytes 196616 | tf_op jit(solution)/shard_map/ppermute | solution.py:34
  174.9 4.3 %collective-permute-start.6 = (f32[1,128,64]{2,1,0:T(8,128)S(1)}, f32[1,128,64]{2,1,0:T(8,128)S(1)}, u32[]{:S(2)}, u32[]{:S(2)}) collective-permute-start(f32[1,128,64]{2,1,0:T(8,128)S(1)} %get-tuple-element.239), channel_id=1, source_target_pairs={{0,4},{4,8},{8,12},{12,16},{16,20},{20,24},{24,28},{28,32},{32,36}... | collective-permute-start | bytes 98312 | tf_op jit(solution)/shard_map/ppermute | solution.py:23
  175.0 8.6 %collective-permute-start.7 = (f32[1,128,64]{2,1,0:T(8,128)S(1)}, f32[1,128,64]{2,1,0:T(8,128)S(1)}, u32[]{:S(2)}, u32[]{:S(2)}) collective-permute-start(f32[1,128,64]{2,1,0:T(8,128)S(1)} %get-tuple-element.238), channel_id=1, source_target_pairs={{4,0},{8,4},{12,8},{16,12},{20,16},{24,20},{28,24},{32,28},{36,32}... | collective-permute-start | bytes 98312 | tf_op jit(solution)/shard_map/ppermute | solution.py:26
  184.4 4.3 %collective-permute-start.8 = (f32[1,128,64]{2,1,0:T(8,128)S(1)}, f32[1,128,64]{2,1,0:T(8,128)S(1)}, u32[]{:S(2)}, u32[]{:S(2)}) collective-permute-start(f32[1,128,64]{2,1,0:T(8,128)S(1)} %get-tuple-element.242), channel_id=1, source_target_pairs={{0,4},{4,8},{8,12},{12,16},{16,20},{20,24},{24,28},{28,32},{32,36}... | collective-permute-start | bytes 98312 | tf_op jit(solution)/shard_map/ppermute | solution.py:23
  184.8 9.4 %collective-permute-start.9 = (f32[1,128,64]{2,1,0:T(8,128)S(1)}, f32[1,128,64]{2,1,0:T(8,128)S(1)}, u32[]{:S(2)}, u32[]{:S(2)}) collective-permute-start(f32[1,128,64]{2,1,0:T(8,128)S(1)} %get-tuple-element.243), channel_id=1, source_target_pairs={{4,0},{8,4},{12,8},{16,12},{20,16},{24,20},{28,24},{32,28},{36,32}... | collective-permute-start | bytes 98312 | tf_op jit(solution)/shard_map/ppermute | solution.py:26
  194.4 11.0 %collective-permute-start.10 = (f32[1,64,256]{2,1,0:T(8,128)S(1)}, f32[1,64,256]{2,1,0:T(8,128)S(1)}, u32[]{:S(2)}, u32[]{:S(2)}) collective-permute-start(f32[1,64,256]{2,1,0:T(8,128)S(1)} %get-tuple-element.236), channel_id=1, source_target_pairs={{0,32},{4,36},{8,40},{12,44},{16,48},{20,52},{24,56},{28,60},{32,6... | collective-permute-start | bytes 196616 | tf_op jit(solution)/shard_map/ppermute | solution.py:34
  198.4 10.1 %collective-permute-start.11 = (f32[1,64,256]{2,1,0:T(8,128)S(1)}, f32[1,64,256]{2,1,0:T(8,128)S(1)}, u32[]{:S(2)}, u32[]{:S(2)}) collective-permute-start(f32[1,64,256]{2,1,0:T(8,128)S(1)} %get-tuple-element.237), channel_id=1, source_target_pairs={{32,0},{36,4},{40,8},{44,12},{48,16},{52,20},{56,24},{60,28},{64,3... | collective-permute-start | bytes 196616 | tf_op jit(solution)/shard_map/ppermute | solution.py:34
  209.6 17.9 %all-to-all-start.1 = ((f32[4,1,256,256]{3,2,1,0:T(8,128)}), f32[4,1,256,256]{3,2,1,0:T(8,128)S(1)}, u32[]{:S(2)}, u32[]{:S(2)}) async-start(f32[4,1,256,256]{3,2,1,0:T(8,128)} %broadcast_in_dim.9), calls=%async_computation.1 | async-start | bytes 2097152 | tf_op jit(solution)/shard_map/all_to_all | solution.py:61
  269.9 1.9 copy-start.1
  333.4 11.4 %collective-permute-start.12 = (f32[1,64,256]{2,1,0:T(8,128)S(1)}, f32[1,64,256]{2,1,0:T(8,128)S(1)}, u32[]{:S(2)}, u32[]{:S(2)}) collective-permute-start(f32[1,64,256]{2,1,0:T(8,128)S(1)} %get-tuple-element.227), channel_id=1, source_target_pairs={{0,32},{4,36},{8,40},{12,44},{16,48},{20,52},{24,56},{28,60},{32,6... | collective-permute-start | bytes 196616 | tf_op jit(solution)/shard_map/ppermute | solution.py:34
  341.4 10.2 %collective-permute-start.13 = (f32[1,64,256]{2,1,0:T(8,128)S(1)}, f32[1,64,256]{2,1,0:T(8,128)S(1)}, u32[]{:S(2)}, u32[]{:S(2)}) collective-permute-start(f32[1,64,256]{2,1,0:T(8,128)S(1)} %get-tuple-element.226), channel_id=1, source_target_pairs={{32,0},{36,4},{40,8},{44,12},{48,16},{52,20},{56,24},{60,28},{64,3... | collective-permute-start | bytes 196616 | tf_op jit(solution)/shard_map/ppermute | solution.py:34
  351.6 4.3 %collective-permute-start.14 = (f32[1,128,64]{2,1,0:T(8,128)S(1)}, f32[1,128,64]{2,1,0:T(8,128)S(1)}, u32[]{:S(2)}, u32[]{:S(2)}) collective-permute-start(f32[1,128,64]{2,1,0:T(8,128)S(1)} %get-tuple-element.235), channel_id=1, source_target_pairs={{0,4},{4,8},{8,12},{12,16},{16,20},{20,24},{24,28},{28,32},{32,36}... | collective-permute-start | bytes 98312 | tf_op jit(solution)/shard_map/ppermute | solution.py:23
  353.0 8.8 %collective-permute-start.15 = (f32[1,128,64]{2,1,0:T(8,128)S(1)}, f32[1,128,64]{2,1,0:T(8,128)S(1)}, u32[]{:S(2)}, u32[]{:S(2)}) collective-permute-start(f32[1,128,64]{2,1,0:T(8,128)S(1)} %get-tuple-element.234), channel_id=1, source_target_pairs={{4,0},{8,4},{12,8},{16,12},{20,16},{24,20},{28,24},{32,28},{36,32}... | collective-permute-start | bytes 98312 | tf_op jit(solution)/shard_map/ppermute | solution.py:26
  362.6 4.3 %collective-permute-start.16 = (f32[1,128,64]{2,1,0:T(8,128)S(1)}, f32[1,128,64]{2,1,0:T(8,128)S(1)}, u32[]{:S(2)}, u32[]{:S(2)}) collective-permute-start(f32[1,128,64]{2,1,0:T(8,128)S(1)} %get-tuple-element.240), channel_id=1, source_target_pairs={{0,4},{4,8},{8,12},{12,16},{16,20},{20,24},{24,28},{28,32},{32,36}... | collective-permute-start | bytes 98312 | tf_op jit(solution)/shard_map/ppermute | solution.py:23
  363.3 8.7 %collective-permute-start.17 = (f32[1,128,64]{2,1,0:T(8,128)S(1)}, f32[1,128,64]{2,1,0:T(8,128)S(1)}, u32[]{:S(2)}, u32[]{:S(2)}) collective-permute-start(f32[1,128,64]{2,1,0:T(8,128)S(1)} %get-tuple-element.241), channel_id=1, source_target_pairs={{4,0},{8,4},{12,8},{16,12},{20,16},{24,20},{28,24},{32,28},{36,32}... | collective-permute-start | bytes 98312 | tf_op jit(solution)/shard_map/ppermute | solution.py:26
  372.1 11.0 %collective-permute-start.18 = (f32[1,64,256]{2,1,0:T(8,128)S(1)}, f32[1,64,256]{2,1,0:T(8,128)S(1)}, u32[]{:S(2)}, u32[]{:S(2)}) collective-permute-start(f32[1,64,256]{2,1,0:T(8,128)S(1)} %get-tuple-element.232), channel_id=1, source_target_pairs={{0,32},{4,36},{8,40},{12,44},{16,48},{20,52},{24,56},{28,60},{32,6... | collective-permute-start | bytes 196616 | tf_op jit(solution)/shard_map/ppermute | solution.py:34
  379.6 10.2 %collective-permute-start.19 = (f32[1,64,256]{2,1,0:T(8,128)S(1)}, f32[1,64,256]{2,1,0:T(8,128)S(1)}, u32[]{:S(2)}, u32[]{:S(2)}) collective-permute-start(f32[1,64,256]{2,1,0:T(8,128)S(1)} %get-tuple-element.233), channel_id=1, source_target_pairs={{32,0},{36,4},{40,8},{44,12},{48,16},{52,20},{56,24},{60,28},{64,3... | collective-permute-start | bytes 196616 | tf_op jit(solution)/shard_map/ppermute | solution.py:34
  391.0 3.7 copy-start.3
  391.0 3.7 copy-start.4
  391.0 18.1 %all-to-all-start.3 = ((f32[4,1,256,256]{3,2,1,0:T(8,128)}), f32[4,1,256,256]{3,2,1,0:T(8,128)S(1)}, u32[]{:S(2)}, u32[]{:S(2)}) async-start(f32[4,1,256,256]{3,2,1,0:T(8,128)} %broadcast_in_dim.10), calls=%async_computation.3 | async-start | bytes 2097152 | tf_op jit(solution)/shard_map/all_to_all | solution.py:61
where the time goes:
time: 416 us; the launch traced here: 410 us
  waiting for transfers between devices  113 us (27%)
  matrix products  99.8 us (24%)
  starting transfers between devices  77.3 us (19%)
  blocking collectives  48.8 us (12%)
  local copies, waits for them, and re-layouts  38.5 us (9%)
  other arithmetic  29.6 us (7%)
    ppermute x10, starting transfers between devices, from_behind(): lax.ppermute(value, axis, [(source, source + steps) for source in range(f...  57.3 us
    dot_general x48, matrix products, product_right(): jnp.einsum('...jk,kl->...jl', operand, matrix, precision=lax.Precision.HI...  50.7 us
    dot_general x48, matrix products, product_left(): jnp.einsum('jk,...kl->...jl', matrix, operand, precision=lax.Precision.HI...  49 us
    ppermute x10, waiting for transfers between devices, from_behind(): lax.ppermute(value, axis, [(source, source + steps) for source in range(f...  40.4 us
    all_to_all x2, blocking collectives, sent_and_summed(): lax.all_to_all(in_blocks(value, dim, length), axis, 0, 0, tiled=True)  34.4 us
    all_to_all x2, waiting for transfers between devices, sent_to_all(): return lax.all_to_all(copies, axis, split_axis=0, concat_axis=0, tiled=True)  28.1 us
    ppermute x5, waiting for transfers between devices, with_halo(): lax.ppermute(lax.slice_in_dim(block, 0, width, axis=dim), axis, backward)  26.3 us
    scatter-add x8, other arithmetic  21 us
  transfers between devices with their start and end apart: 22, of which 22 were waited for; matrix products, arithmetic and copies ran while one was open for 1% of the time, Pallas kernels for 0%

commit v1 on v0

v1 whole, which is shorter than its diff:
```python
import functools
import math

import jax
import jax.numpy as jnp
import numpy as np
from jax import lax
from jax.experimental import pallas as pl
from jax.experimental.pallas import tpu as pltpu
from jax.sharding import PartitionSpec as P

K = 128
HALO = 64
EXT = 256
STEPS = 2
TILE_COLS = 8
WAVES = 8

MESH = pl.DeviceIdType.MESH
f32 = jnp.float32
bf16 = jnp.bfloat16


def tables():
    index = np.arange(K)
    angle = (index[:, None] * index[None, :] % K) * (2.0 * math.pi / K)
    cos = np.cos(angle) / math.sqrt(K)
    sin = -np.sin(angle) / math.sqrt(K)
    out = []
    for sign in (1.0, -1.0):
        full = np.block([[cos, sign * sin], [-sign * sin, cos]]).astype(np.float32)
        hi = full.astype(bf16)
        lo = (full - hi.astype(np.float32)).astype(bf16)
        out.append(np.concatenate([hi, lo], axis=0))
    return np.stack(out)


def halves(x):
    return x[:, :K], x[:, K:]


def both(re, im):
    return jnp.concatenate([re, im], axis=1)


def times(x, table):
    hi = x.astype(bf16)
    lo = (x - hi.astype(f32)).astype(bf16)
    return jnp.dot(
        jnp.concatenate([hi, lo, hi], axis=1), table, preferred_element_type=f32
    )


def turned(x):
    re, im = halves(x)
    return both(re.T, im.T)


def mul(a, b):
    ar, ai = a
    br, bi = b
    return ar * br - ai * bi, ar * bi + ai * br


def conj_mul(a, b):
    ar, ai = a
    br, bi = b
    return ar * br + ai * bi, ar * bi - ai * br


def swap_lanes(x):
    return pltpu.roll(x, HALO, axis=1)


def low_lanes(rows):
    return lax.broadcasted_iota(jnp.int32, (rows, K), 1) < HALO


def pack(upper, lower):
    keep = low_lanes(upper.shape[0])
    return (
        jnp.where(keep, upper, swap_lanes(lower)),
        jnp.where(keep, swap_lanes(upper), lower),
    )


def unpack(low, high):
    keep = low_lanes(low.shape[0])
    return (
        jnp.where(keep, low, swap_lanes(high)),
        jnp.where(keep, swap_lanes(low), high),
    )


def kernel(
    pos,
    obj_in,
    probe_in,
    phase_in,
    meas_in,
    table_in,
    obj_out,
    int_out,
    table,
    phase,
    probe,
    meas,
    plane_now,
    wide,
    win_send,
    win,
    psi,
    mid,
    work,
    prop,
    part,
    part_recv,
    inten,
    grad,
    grad_recv,
    placed,
    edge_send,
    edge_recv,
    corner_send,
    corner_recv,
    in_sem,
    out_sem,
    s_probe, r_probe,
    s_win, r_win,
    s_part, r_part,
    s_int, r_int,
    s_grad, r_grad,
    s_edge, r_edge,
    s_corner, r_corner,
    s_fin, r_fin,
):
    tiles = lax.axis_size("tile")
    t = lax.axis_index("tile")
    m = lax.axis_index("mode")
    core = m % 2
    chip = m // 2
    plane = core * 2 + chip

    def tile_at(rows, cols):
        return (lax.rem(t + tiles + rows * TILE_COLS + cols, tiles), m)

    up, down, left, right = tile_at(-1, 0), tile_at(1, 0), tile_at(0, -1), tile_at(0, 1)
    up_left, up_right = tile_at(-1, -1), tile_at(-1, 1)
    down_left, down_right = tile_at(1, -1), tile_at(1, 1)
    mate = [None, m + 1 - 2 * core, lax.rem(m + 2, 4), 3 - m]
    group = [None] + [(t, mate[j]) for j in (1, 2, 3)]

    def plane_of(who):
        return (who % 2) * 2 + who // 2

    def remote(src, dst, send, recv, to):
        return pltpu.make_async_remote_copy(
            src_ref=src, dst_ref=dst, send_sem=send, recv_sem=recv,
            device_id=to, device_id_type=MESH,
        )

    load_obj = pltpu.make_async_copy(obj_in.at[0, core, chip], plane_now, in_sem.at[0])
    load_probe = pltpu.make_async_copy(probe_in, probe.at[pl.ds(0, 4)], in_sem.at[1])
    load_phase = pltpu.make_async_copy(phase_in, phase, in_sem.at[2])
    load_meas = pltpu.make_async_copy(meas_in, meas, in_sem.at[3])
    load_table = pltpu.make_async_copy(table_in, table, in_sem.at[4])
    for copy in (load_obj, load_probe, load_phase, load_meas, load_table):
        copy.start()

    barrier = pltpu.get_barrier_semaphore()
    partners = [up, down, left, right, up_left, up_right, down_left, down_right] + group[1:]
    for who in partners:
        pl.semaphore_signal(barrier, inc=1, device_id=who, device_id_type=MESH)
    load_obj.wait()

    def row_ok():
        row = lax.broadcasted_iota(jnp.int32, (EXT, K), 0)
        first = jnp.where(t >= TILE_COLS, 0, HALO)
        last = jnp.where(t < tiles - TILE_COLS, EXT, EXT - HALO)
        return jnp.logical_and(row >= first, row < last)

    def exchange(e, top, bottom, side_low, side_high, corners, sides):
        low_side, high_side, tl, th, bl, bh = sides
        copies = []
        for i, (block, to) in enumerate(zip(corners, (tl, th, bl, bh))):
            corner_send[e, i] = block
            copies.append(remote(corner_send.at[e, i], corner_recv.at[e, i], s_corner.at[e, i], r_corner.at[e, i], to))
            copies[-1].start()
        for i, (block, to) in enumerate(zip((top, bottom, side_low, side_high), (up, down, low_side, high_side))):
            edge_send[e, i] = block
            copies.append(remote(edge_send.at[e, i], edge_recv.at[e, i], s_edge.at[e, i], r_edge.at[e, i], to))
            copies[-1].start()
        return copies

    def send_edges(e):
        x = plane_now[...]
        side_low, side_high = pack(x[:HALO], x[HALO:])
        t_low, t_high = pack(x[:32], x[32:64])
        b_low, b_high = pack(x[64:96], x[96:])
        return exchange(
            e, x[:HALO], x[HALO:], side_low, side_high, (t_low, t_high, b_low, b_high),
            (left, right, up_left, up_right, down_left, down_right),
        )

    def take_edges(e, copies):
        wide[0, HALO : HALO + K] = plane_now[...]
        for copy in copies:
            copy.wait()
        first = jnp.where(t >= TILE_COLS, 1.0, 0.0)
        last = jnp.where(t < tiles - TILE_COLS, 1.0, 0.0)
        wide[0, HALO + K :] = edge_recv[e, 0] * last
        wide[0, :HALO] = edge_recv[e, 1] * first
        a, b = unpack(edge_recv[e, 2], edge_recv[e, 3])
        wide[1, HALO:K] = a
        wide[1, K : K + HALO] = b
        a, b = unpack(corner_recv[e, 0], corner_recv[e, 1])
        wide[1, 192:224] = a * last
        wide[1, 224:256] = b * last
        a, b = unpack(corner_recv[e, 2], corner_recv[e, 3])
        wide[1, 0:32] = a * first
        wide[1, 32:64] = b * first

    def fold(e, inner, outer):
        side_low, side_high = pack(outer[HALO:K], outer[K : K + HALO])
        t_low, t_high = pack(outer[0:32], outer[32:64])
        b_low, b_high = pack(outer[192:224], outer[224:256])
        copies = exchange(
            e, inner[:HALO], inner[K + HALO :], side_low, side_high, (t_low, t_high, b_low, b_high),
            (right, left, up_right, up_left, down_right, down_left),
        )
        for copy in copies:
            copy.wait()
        a, b = unpack(edge_recv[e, 2], edge_recv[e, 3])
        top = inner[HALO:K] + edge_recv[e, 1] + a
        bottom = inner[K : K + HALO] + edge_recv[e, 0] + b
        ta, tb = unpack(corner_recv[e, 2], corner_recv[e, 3])
        ba, bb = unpack(corner_recv[e, 0], corner_recv[e, 1])
        top = top + jnp.concatenate([ta, tb], axis=0)
        bottom = bottom + jnp.concatenate([ba, bb], axis=0)
        return jnp.concatenate([top, bottom], axis=0)

    def window(n, q):
        r = pos[n * 2 + q, 0]
        c = pos[n * 2 + q, 1]
        rows = both(wide[0, pl.ds(r, K), :], wide[1, pl.ds(r, K), :])
        return pltpu.roll(rows, lax.rem(EXT + HALO - c, EXT), axis=1)[:, :K]

    def send_windows(n):
        copies = [
            remote(win_send.at[n, 0], win.at[n, plane], s_win.at[n, 0], r_win.at[n, 0], group[1]),
            remote(win_send.at[n, 1], win.at[n, plane], s_win.at[n, 1], r_win.at[n, 1], group[2]),
            remote(win_send.at[n, 1], win.at[n, plane], s_win.at[n, 2], r_win.at[n, 2], group[3]),
        ]
        win_send[n, 1] = window(n, 1 - chip)
        copies[1].start()
        copies[2].start()
        own = window(n, chip)
        win_send[n, 0] = own
        copies[0].start()
        win[n, plane] = own
        return copies

    def place(n, q, g):
        r = pos[n * 2 + q, 0]
        c = pos[n * 2 + q, 1]
        padded = both(g, jnp.zeros((K, K), f32))
        a, b = halves(pltpu.roll(padded, lax.rem(c + EXT - HALO, EXT), axis=1))
        placed[0, K : 2 * K] = a
        placed[1, K : 2 * K] = b
        rows = pl.ds(K - r, EXT)
        return placed[0, rows, :], placed[1, rows, :]

    def tab(which):
        hi = table[which, 0:EXT]
        return jnp.concatenate([hi, hi, table[which, EXT:]], axis=0)

    pl.semaphore_wait(barrier, len(partners))
    send_probe = remote(probe.at[pl.ds(0, 4)], probe.at[pl.ds(4, 4)], s_probe.at[0], r_probe.at[0], group[2])
    pending = []
    halo_copies = send_edges(0)
    load_probe.wait()
    send_probe.start()
    load_phase.wait()
    angle = phase[...].T
    prop[0] = jnp.cos(angle)
    prop[1] = jnp.sin(angle)
    for half in range(2):
        placed[half] = jnp.zeros((384, K), f32)
    take_edges(0, halo_copies)
    win_copies = send_windows(0)
    load_meas.wait()
    load_table.wait()

    for n in range(STEPS):
        meas_n = meas[n * 2 + chip].T

        def f1(j):
            re, im = mul((1.0 + win[n, 0], win[n, 1]), (probe[j, 0], probe[j, 1]))
            work[j] = turned(times(both(re, im), tab(0)))

        def f2(j):
            y = halves(times(work[j], tab(0)))
            work[j] = both(*mul((prop[0], prop[1]), y))

        def f3(j):
            work[j] = turned(times(work[j], tab(1)))

        def f4(j):
            y = times(work[j], tab(1))
            mid[j] = y
            work[j] = both(*mul((1.0 + win[n, 2], win[n, 3]), halves(y)))

        def f5(j):
            work[j] = turned(times(work[j], tab(0)))

        def f6(j):
            y = times(work[j], tab(0))
            psi[j] = y
            re, im = halves(y)
            if j == 0:
                part[n] = re * re + im * im
            else:
                part[n] += re * re + im * im

        for copy in win_copies:
            copy.wait()
        groups = ((0, 1, 2, 3), (4, 5, 6, 7)) if n == 0 else (range(WAVES),)
        for g, waves in enumerate(groups):
            if n == 0 and g == 1:
                send_probe.wait()
            for stage in (f1, f2, f3, f4, f5, f6):
                for j in waves:
                    stage(j)

        send_part = remote(part.at[n], part_recv.at[n], s_part.at[n], r_part.at[n], group[1])
        send_part.start()
        send_part.wait()
        intensity = part[n] + part_recv[n]
        residual = intensity - meas_n
        inten[n] = intensity.T

        def b1(j):
            work[j] = turned(times(both(residual, residual) * psi[j], tab(1)))

        def b2(j):
            g = halves(times(work[j], tab(1)))
            re, im = conj_mul(halves(mid[j]), g)
            if j == 0:
                grad[n, 2] = re
                grad[n, 3] = im
            else:
                grad[n, 2] += re
                grad[n, 3] += im
            work[j] = both(*conj_mul((1.0 + win[n, 2], win[n, 3]), g))

        def b3(j):
            work[j] = turned(times(work[j], tab(0)))

        def b4(j):
            y = halves(times(work[j], tab(0)))
            work[j] = both(*conj_mul((prop[0], prop[1]), y))

        def b5(j):
            work[j] = turned(times(work[j], tab(1)))

        def b6(j):
            g = halves(times(work[j], tab(1)))
            re, im = conj_mul((probe[j, 0], probe[j, 1]), g)
            if j == 0:
                grad[n, 0] = re
                grad[n, 1] = im
            else:
                grad[n, 0] += re
                grad[n, 1] += im

        grad_copies = [
            remote(
                grad.at[n, plane_of(mate[j])], grad_recv.at[n, j - 1],
                s_grad.at[n, j - 1], r_grad.at[n, j - 1], group[j],
            )
            for j in (1, 2, 3)
        ]

        for stage in (b1, b2):
            for j in range(WAVES):
                stage(j)

        @pl.when(core == 1)
        def _():
            grad_copies[1].start()

        @pl.when(core == 0)
        def _():
            grad_copies[2].start()
            grad_copies[0].start()

        for stage in (b3, b4, b5, b6):
            for j in range(WAVES):
                stage(j)

        @pl.when(core == 0)
        def _():
            grad_copies[1].start()

        @pl.when(core == 1)
        def _():
            grad_copies[2].start()
            grad_copies[0].start()

        slot = n * 2 + chip
        keep_int = pltpu.make_async_copy(inten.at[n], int_out.at[slot], out_sem.at[n])
        send_int = remote(inten.at[n], int_out.at[slot], s_int.at[n], r_int.at[n], group[2])

        for copy in grad_copies:
            copy.wait()
        inner, outer = place(n, chip, grad[n, plane] + grad_recv[n, 0])
        inner2, outer2 = place(n, 1 - chip, grad_recv[n, 1] + grad_recv[n, 2])
        ok = row_ok()
        inner = jnp.where(ok, inner + inner2, 0.0)
        outer = jnp.where(ok, outer + outer2, 0.0)
        keep_int.start()
        total = fold(1 + 2 * n, inner, outer)
        send_int.start()
        pending += [keep_int, send_int]
        plane_now[...] = plane_now[...] - total
        if n + 1 < STEPS:
            take_edges(2 + 2 * n, send_edges(2 + 2 * n))
            win_copies = send_windows(n + 1)

    there = obj_out.at[0, core, chip]
    for j in (3, 2, 1):
        copy = remote(plane_now, there, s_fin.at[j - 1], r_fin.at[j - 1], group[j])
        copy.start()
        pending.append(copy)
    keep_obj = pltpu.make_async_copy(plane_now, there, out_sem.at[2])
    keep_obj.start()
    pending.append(keep_obj)
    for copy in pending:
        copy.wait()


def local(object_tiles, probe, propagator_phase, measured, positions):
    anywhere = pl.BlockSpec(memory_space=pl.ANY)
    dma = pltpu.SemaphoreType.DMA
    V = pltpu.VMEM
    scratch = [
        V((2, 2 * EXT, EXT), bf16),
        V((K, K), f32),
        V((WAVES, 2, K, K), f32),
        V((4, K, K), f32),
        V((K, K), f32),
        V((2, EXT, K), f32),
        V((2, 2, K, K), f32),
        V((2, 4, K, K), f32),
        V((WAVES, K, EXT), f32),
        V((WAVES, K, EXT), f32),
        V((WAVES, K, EXT), f32),
        V((2, K, K), f32),
        V((2, K, K), f32),
        V((2, K, K), f32),
        V((2, K, K), f32),
        V((2, 4, K, K), f32),
        V((2, 3, K, K), f32),
        V((2, 384, K), f32),
        V((4, 4, HALO, K), f32),
        V((4, 4, HALO, K), f32),
        V((4, 4, 32, K), f32),
        V((4, 4, 32, K), f32),
        dma((5,)),
        dma((3,)),
        dma((1,)), dma((1,)),
        dma((2, 3)), dma((2, 3)),
        dma((2,)), dma((2,)),
        dma((2,)), dma((2,)),
        dma((2, 3)), dma((2, 3)),
        dma((4, 4)), dma((4, 4)),
        dma((4, 4)), dma((4, 4)),
        dma((3,)), dma((3,)),
    ]
    return pl.pallas_call(
        kernel,
        name="ptycho",
        out_shape=(
            jax.ShapeDtypeStruct(object_tiles.shape, f32),
            jax.ShapeDtypeStruct(measured.shape, f32),
        ),
        in_specs=[pl.BlockSpec(memory_space=pltpu.SMEM)] + [anywhere] * 5,
        out_specs=(anywhere, anywhere),
        scratch_shapes=scratch,
        compiler_params=pltpu.CompilerParams(
            collective_id=0, has_side_effects=True, vmem_limit_bytes=48 * 1024 * 1024
        ),
    )(positions, object_tiles, probe, propagator_phase, measured, jnp.asarray(tables()))


def solution(mesh):
    return jax.shard_map(
        local,
        mesh=mesh,
        in_specs=(
            P("tile", None, None, None, None),
            P("mode", None, None, None),
            P(),
            P("tile", None, None),
            P("tile", None),
        ),
        out_specs=(P("tile", None, None, None, None), P("tile", None, None)),
        check_vma=False,
    )
```

time: 416 us -> 100 us (0.24)
  the two profiles are of different devices: /device:TPU:78 before, /device:TPU:1 now
where the time goes in v1:
time: 100 us; the launch traced here: 99.9 us
  Pallas kernels  92.3 us (92%)
  local copies, waits for them, and re-layouts  6.99 us (7%)
    pallas_call x1, Pallas kernels, local(): pl.pallas_call(kernel, name='ptycho', out_shape=(jax.ShapeDtypeStruct(obj...  92.3 us
    unnamed x13, local copies, waits for them, and re-layouts  6.99 us

profile of v1, /device:TPU:1, one launch (start us, length us, event | category | flops | bytes accessed | tf_op | source)
XLA Modules:
  0.0 99.9 jit_solution(14792575488747966584)
XLA Ops:
  0.6 0.8 copy.8.pos
  1.4 0.0 copy-start
  1.4 1.0 %copy-done = f32[4,2,128,128]{3,2,1,0:T(8,128)S(1)} copy-done((f32[4,2,128,128]{3,2,1,0:T(8,128)S(1)}, f32[4,2,128,128]{3,2,1,0:T(8,128)}, u32[]{:S(2)}) %copy-start) | copy-done | bytes 524312
  2.4 0.0 copy-start.1
  2.4 1.0 %copy-done.1 = bf16[2,512,256]{2,1,0:T(8,128)(2,1)S(1)} copy-done((bf16[2,512,256]{2,1,0:T(8,128)(2,1)S(1)}, bf16[2,512,256]{2,1,0:T(8,128)(2,1)}, u32[]{:S(2)}) %copy-start.1) | copy-done | bytes 524312
  3.5 0.0 copy-start.2
  3.5 0.9 copy-done.2
  4.4 0.0 copy-start.3
  4.4 0.9 copy-done.3
  5.4 0.0 copy-start.4
  5.4 0.8 copy-done.4
  6.2 92.3 %ptycho.1 = (f32[1,2,2,128,128]{4,3,2,1,0:T(8,128)S(1)}, f32[4,128,128]{2,1,0:T(8,128)S(1)}) custom-call(s32[4,2]{1,0:T(4,128)S(1)} %copy.8.pos, f32[1,2,2,128,128]{4,3,2,1,0:T(8,128)S(1)} %copy-done.2, f32[4,2,128,128]{3,2,1,0:T(8,128)S(1)} %copy-done, f32[128,128]{1,0:T(8,128)S(1)} %copy-done.4, f32[4,128,128]{2,1,0:T(8,128)S(1)} %copy-done.3, ...), custom_call_target="tpu_custom_call" | custom-call | tf_op jit(solution)/shard_map/ptycho/pallas_call | solution.py:480
  98.5 0.7 copy.11
  99.2 0.7 copy.12
Async XLA Ops:
  1.4 1.0 %copy-start = (f32[4,2,128,128]{3,2,1,0:T(8,128)S(1)}, f32[4,2,128,128]{3,2,1,0:T(8,128)}, u32[]{:S(2)}) copy-start(f32[4,2,128,128]{3,2,1,0:T(8,128)} %probe_in.1) | copy-start | bytes 1572868
  2.4 1.0 %copy-start.1 = (bf16[2,512,256]{2,1,0:T(8,128)(2,1)S(1)}, bf16[2,512,256]{2,1,0:T(8,128)(2,1)}, u32[]{:S(2)}) copy-start(bf16[2,512,256]{2,1,0:T(8,128)(2,1)} %constant.2.clone.table_in) | copy-start | bytes 1572868
  3.5 0.9 copy-start.2
  4.4 0.9 copy-start.3
  5.4 0.8 copy-start.4

commit v2 on v1

--- a/solution.py
+++ b/solution.py
@@ -139,10 +139,15 @@
     m = lax.axis_index("mode")
     core = m % 2
     chip = m // 2
-    plane = core * 2 + chip
+    comp = (chip + t // TILE_COLS) % 2
+    plane = core * 2 + comp
+    pattern = [core, chip]
+    same = [2, 1]
+    swap = [1, 2]
 
     def tile_at(rows, cols):
-        return (lax.rem(t + tiles + rows * TILE_COLS + cols, tiles), m)
+        there = lax.rem(t + tiles + rows * TILE_COLS + cols, tiles)
+        return (there, (comp + there // TILE_COLS) % 2 * 2 + core)
 
     up, down, left, right = tile_at(-1, 0), tile_at(1, 0), tile_at(0, -1), tile_at(0, 1)
     up_left, up_right = tile_at(-1, -1), tile_at(-1, 1)
@@ -151,7 +156,7 @@
     group = [None] + [(t, mate[j]) for j in (1, 2, 3)]
 
     def plane_of(who):
-        return (who % 2) * 2 + who // 2
+        return (who % 2) * 2 + (who // 2 + t // TILE_COLS) % 2
 
     def remote(src, dst, send, recv, to):
         return pltpu.make_async_remote_copy(
@@ -159,19 +164,18 @@
             device_id=to, device_id_type=MESH,
         )
 
-    load_obj = pltpu.make_async_copy(obj_in.at[0, core, chip], plane_now, in_sem.at[0])
+    load_plane = pltpu.make_async_copy(obj_in.at[0, core, comp], plane_now, in_sem.at[0])
     load_probe = pltpu.make_async_copy(probe_in, probe.at[pl.ds(0, 4)], in_sem.at[1])
     load_phase = pltpu.make_async_copy(phase_in, phase, in_sem.at[2])
     load_meas = pltpu.make_async_copy(meas_in, meas, in_sem.at[3])
     load_table = pltpu.make_async_copy(table_in, table, in_sem.at[4])
-    for copy in (load_obj, load_probe, load_phase, load_meas, load_table):
+    for copy in (load_plane, load_probe, load_phase, load_meas, load_table):
         copy.start()
 
     barrier = pltpu.get_barrier_semaphore()
     partners = [up, down, left, right, up_left, up_right, down_left, down_right] + group[1:]
     for who in partners:
         pl.semaphore_signal(barrier, inc=1, device_id=who, device_id_type=MESH)
-    load_obj.wait()
 
     def row_ok():
         row = lax.broadcasted_iota(jnp.int32, (EXT, K), 0)
@@ -192,8 +196,12 @@
             copies[-1].start()
         return copies
 
-    def send_edges(e):
-        x = plane_now[...]
+    def arrived(copies):
+        for copy in copies:
+            copy.wait_recv()
+        sent.extend(copies)
+
+    def send_edges(e, x):
         side_low, side_high = pack(x[:HALO], x[HALO:])
         t_low, t_high = pack(x[:32], x[32:64])
         b_low, b_high = pack(x[64:96], x[96:])
@@ -202,17 +210,18 @@
             (left, right, up_left, up_right, down_left, down_right),
         )
 
-    def take_edges(e, copies):
-        wide[0, HALO : HALO + K] = plane_now[...]
-        for copy in copies:
-            copy.wait()
+    def take_edges(e, x, copies):
+        wide[0, HALO : HALO + K] = x
         first = jnp.where(t >= TILE_COLS, 1.0, 0.0)
         last = jnp.where(t < tiles - TILE_COLS, 1.0, 0.0)
-        wide[0, HALO + K :] = edge_recv[e, 0] * last
-        wide[0, :HALO] = edge_recv[e, 1] * first
+        arrived(copies[6:])
         a, b = unpack(edge_recv[e, 2], edge_recv[e, 3])
         wide[1, HALO:K] = a
         wide[1, K : K + HALO] = b
+        arrived(copies[4:6])
+        wide[0, HALO + K :] = edge_recv[e, 0] * last
+        wide[0, :HALO] = edge_recv[e, 1] * first
+        arrived(copies[:4])
         a, b = unpack(corner_recv[e, 0], corner_recv[e, 1])
         wide[1, 192:224] = a * last
         wide[1, 224:256] = b * last
@@ -220,7 +229,7 @@
         wide[1, 0:32] = a * first
         wide[1, 32:64] = b * first
 
-    def fold(e, inner, outer):
+    def fold(e, inner, outer, after=()):
         side_low, side_high = pack(outer[HALO:K], outer[K : K + HALO])
         t_low, t_high = pack(outer[0:32], outer[32:64])
         b_low, b_high = pack(outer[192:224], outer[224:256])
@@ -228,11 +237,14 @@
             e, inner[:HALO], inner[K + HALO :], side_low, side_high, (t_low, t_high, b_low, b_high),
             (right, left, up_right, up_left, down_right, down_left),
         )
-        for copy in copies:
-            copy.wait()
+        for copy in after:
+            copy.start()
+        arrived(copies[6:])
         a, b = unpack(edge_recv[e, 2], edge_recv[e, 3])
+        arrived(copies[4:6])
         top = inner[HALO:K] + edge_recv[e, 1] + a
         bottom = inner[K : K + HALO] + edge_recv[e, 0] + b
+        arrived(copies[:4])
         ta, tb = unpack(corner_recv[e, 2], corner_recv[e, 3])
         ba, bb = unpack(corner_recv[e, 0], corner_recv[e, 1])
         top = top + jnp.concatenate([ta, tb], axis=0)
@@ -240,29 +252,35 @@
         return jnp.concatenate([top, bottom], axis=0)
 
     def window(n, q):
-        r = pos[n * 2 + q, 0]
-        c = pos[n * 2 + q, 1]
+        r = pos[0, n * 2 + q]
+        c = pos[1, n * 2 + q]
         rows = both(wide[0, pl.ds(r, K), :], wide[1, pl.ds(r, K), :])
         return pltpu.roll(rows, lax.rem(EXT + HALO - c, EXT), axis=1)[:, :K]
 
     def send_windows(n):
         copies = [
-            remote(win_send.at[n, 0], win.at[n, plane], s_win.at[n, 0], r_win.at[n, 0], group[1]),
-            remote(win_send.at[n, 1], win.at[n, plane], s_win.at[n, 1], r_win.at[n, 1], group[2]),
-            remote(win_send.at[n, 1], win.at[n, plane], s_win.at[n, 2], r_win.at[n, 2], group[3]),
+            remote(
+                win_send.at[n, 0 if j == same[n] else 1], win.at[n, plane],
+                s_win.at[n, j - 1], r_win.at[n, j - 1], group[j],
+            )
+            for j in (1, 2, 3)
         ]
-        win_send[n, 1] = window(n, 1 - chip)
-        copies[1].start()
+        own = window(n, pattern[n])
+        if same[n] == 2:
+            win_send[n, 0] = own
+            copies[1].start()
+        win_send[n, 1] = window(n, 1 - pattern[n])
         copies[2].start()
-        own = window(n, chip)
-        win_send[n, 0] = own
-        copies[0].start()
+        copies[swap[n] - 1].start()
+        if same[n] == 1:
+            win_send[n, 0] = own
+            copies[0].start()
         win[n, plane] = own
         return copies
 
     def place(n, q, g):
-        r = pos[n * 2 + q, 0]
-        c = pos[n * 2 + q, 1]
+        r = pos[0, n * 2 + q]
+        c = pos[1, n * 2 + q]
         padded = both(g, jnp.zeros((K, K), f32))
         a, b = halves(pltpu.roll(padded, lax.rem(c + EXT - HALO, EXT), axis=1))
         placed[0, K : 2 * K] = a
@@ -275,27 +293,51 @@
         return jnp.concatenate([hi, hi, table[which, EXT:]], axis=0)
 
     pl.semaphore_wait(barrier, len(partners))
-    send_probe = remote(probe.at[pl.ds(0, 4)], probe.at[pl.ds(4, 4)], s_probe.at[0], r_probe.at[0], group[2])
+    probe_copies = [
+        remote(probe.at[pl.ds(0, 4)], probe.at[pl.ds(4, 4)], s_probe.at[0], r_probe.at[0], group[1]),
+    ] + [
+        remote(probe.at[i], probe.at[8 + i], s_probe.at[1 + i], r_probe.at[1 + i], group[2])
+        for i in range(4)
+    ]
+    sent = []
     pending = []
-    halo_copies = send_edges(0)
+    load_plane.wait()
+    first_copies = send_edges(0, plane_now[...])
     load_probe.wait()
-    send_probe.start()
+    probe_copies[0].start()
     load_phase.wait()
     angle = phase[...].T
     prop[0] = jnp.cos(angle)
     prop[1] = jnp.sin(angle)
     for half in range(2):
         placed[half] = jnp.zeros((384, K), f32)
-    take_edges(0, halo_copies)
-    win_copies = send_windows(0)
     load_meas.wait()
     load_table.wait()
+    take_edges(0, plane_now[...], first_copies)
+    win_copies = send_windows(0)
 
     for n in range(STEPS):
-        meas_n = meas[n * 2 + chip].T
+        meas_n = meas[n * 2 + pattern[n]].T
+
+        def mode(j):
+            at = j if n == 0 or j < 4 else j + 4
+            return probe[at, 0], probe[at, 1]
+
+        def wait_windows(n, s):
+            @pl.when(core == s)
+            def _():
+                win_copies[1].wait_recv()
+
+            @pl.when(core != s)
+            def _():
+                win_copies[0].wait_recv()
+                win_copies[2].wait_recv()
+
+            if s == 1:
+                sent.extend(win_copies)
 
         def f1(j):
-            re, im = mul((1.0 + win[n, 0], win[n, 1]), (probe[j, 0], probe[j, 1]))
+            re, im = mul((1.0 + win[n, 0], win[n, 1]), mode(j))
             work[j] = turned(times(both(re, im), tab(0)))
 
         def f2(j):
@@ -322,19 +364,22 @@
             else:
                 part[n] += re * re + im * im
 
-        for copy in win_copies:
-            copy.wait()
-        groups = ((0, 1, 2, 3), (4, 5, 6, 7)) if n == 0 else (range(WAVES),)
-        for g, waves in enumerate(groups):
-            if n == 0 and g == 1:
-                send_probe.wait()
-            for stage in (f1, f2, f3, f4, f5, f6):
-                for j in waves:
-                    stage(j)
-
-        send_part = remote(part.at[n], part_recv.at[n], s_part.at[n], r_part.at[n], group[1])
+        if n == 0:
+            probe_copies[1].start()
+        arrived(probe_copies[1:] if n else probe_copies[:1])
+        for stage in (f1, f2, f3, f4, f5, f6):
+            if stage is f1:
+                wait_windows(n, 0)
+            if stage is f4:
+                wait_windows(n, 1)
+            for j in range(WAVES):
+                stage(j)
+
+        send_part = remote(part.at[n], part_recv.at[n], s_part.at[n], r_part.at[n], group[same[n]])
         send_part.start()
-        send_part.wait()
+        arrived([send_part])
+        if n == 0:
+            probe_copies[2].start()
         intensity = part[n] + part_recv[n]
         residual = intensity - meas_n
         inten[n] = intensity.T
@@ -365,7 +410,7 @@
 
         def b6(j):
             g = halves(times(work[j], tab(1)))
-            re, im = conj_mul((probe[j, 0], probe[j, 1]), g)
+            re, im = conj_mul(mode(j), g)
             if j == 0:
                 grad[n, 0] = re
                 grad[n, 1] = im
@@ -407,27 +452,31 @@
             grad_copies[2].start()
             grad_copies[0].start()
 
-        slot = n * 2 + chip
+        slot = n * 2 + pattern[n]
         keep_int = pltpu.make_async_copy(inten.at[n], int_out.at[slot], out_sem.at[n])
-        send_int = remote(inten.at[n], int_out.at[slot], s_int.at[n], r_int.at[n], group[2])
-
-        for copy in grad_copies:
-            copy.wait()
-        inner, outer = place(n, chip, grad[n, plane] + grad_recv[n, 0])
-        inner2, outer2 = place(n, 1 - chip, grad_recv[n, 1] + grad_recv[n, 2])
+        send_int = remote(inten.at[n], int_out.at[slot], s_int.at[n], r_int.at[n], group[swap[n]])
+
+        a, b = same[n] - 1, swap[n] - 1
+        arrived([grad_copies[0], grad_copies[a]] if a else [grad_copies[0]])
+        inner, outer = place(n, pattern[n], grad[n, plane] + grad_recv[n, a])
+        arrived([grad_copies[2]] if a else grad_copies[1:])
+        inner2, outer2 = place(n, 1 - pattern[n], grad_recv[n, b] + grad_recv[n, 2])
         ok = row_ok()
         inner = jnp.where(ok, inner + inner2, 0.0)
         outer = jnp.where(ok, outer + outer2, 0.0)
         keep_int.start()
-        total = fold(1 + 2 * n, inner, outer)
+        total = fold(1 + 2 * n, inner, outer, probe_copies[3 + n : 4 + n] if n == 0 else [])
         send_int.start()
         pending += [keep_int, send_int]
         plane_now[...] = plane_now[...] - total
         if n + 1 < STEPS:
-            take_edges(2 + 2 * n, send_edges(2 + 2 * n))
+            x = plane_now[...]
+            edges = send_edges(2 + 2 * n, x)
+            probe_copies[4].start()
+            take_edges(2 + 2 * n, x, edges)
             win_copies = send_windows(n + 1)
 
-    there = obj_out.at[0, core, chip]
+    there = obj_out.at[0, core, comp]
     for j in (3, 2, 1):
         copy = remote(plane_now, there, s_fin.at[j - 1], r_fin.at[j - 1], group[j])
         copy.start()
@@ -435,6 +484,8 @@
     keep_obj = pltpu.make_async_copy(plane_now, there, out_sem.at[2])
     keep_obj.start()
     pending.append(keep_obj)
+    for copy in sent:
+        copy.wait_send()
     for copy in pending:
         copy.wait()
 
@@ -446,7 +497,7 @@
     scratch = [
         V((2, 2 * EXT, EXT), bf16),
         V((K, K), f32),
-        V((WAVES, 2, K, K), f32),
+        V((12, 2, K, K), f32),
         V((4, K, K), f32),
         V((K, K), f32),
         V((2, EXT, K), f32),
@@ -468,7 +519,7 @@
         V((4, 4, 32, K), f32),
         dma((5,)),
         dma((3,)),
-        dma((1,)), dma((1,)),
+        dma((5,)), dma((5,)),
         dma((2, 3)), dma((2, 3)),
         dma((2,)), dma((2,)),
         dma((2,)), dma((2,)),
@@ -477,7 +528,7 @@
         dma((4, 4)), dma((4, 4)),
         dma((3,)), dma((3,)),
     ]
-    return pl.pallas_call(
+    outs = pl.pallas_call(
         kernel,
         name="ptycho",
         out_shape=(
@@ -488,9 +539,35 @@
         out_specs=(anywhere, anywhere),
         scratch_shapes=scratch,
         compiler_params=pltpu.CompilerParams(
-            collective_id=0, has_side_effects=True, vmem_limit_bytes=48 * 1024 * 1024
+            collective_id=0, has_side_effects=True
         ),
-    )(positions, object_tiles, probe, propagator_phase, measured, jnp.asarray(tables()))
+    )(positions.T, object_tiles, probe, propagator_phase, measured, jnp.asarray(tables()))
+    return pl.pallas_call(
+        hand_over,
+        name="hand_over",
+        out_shape=tuple(jax.ShapeDtypeStruct(x.shape, f32) for x in outs),
+        in_specs=[anywhere] * 2,
+        out_specs=(anywhere, anywhere),
+        scratch_shapes=[V(x.shape, f32) for x in outs] + [dma((2,)), dma((2,))],
+    )(*outs)
+
+
+def hand_over(obj_in, int_in, obj_out, int_out, obj, inten, in_sem, out_sem):
+    ins = [
+        pltpu.make_async_copy(obj_in, obj, in_sem.at[0]),
+        pltpu.make_async_copy(int_in, inten, in_sem.at[1]),
+    ]
+    outs = [
+        pltpu.make_async_copy(obj, obj_out, out_sem.at[0]),
+        pltpu.make_async_copy(inten, int_out, out_sem.at[1]),
+    ]
+    for copy in ins:
+        copy.start()
+    for copy, out in zip(ins, outs):
+        copy.wait()
+        out.start()
+    for out in outs:
+        out.wait()
 
 
 def solution(mesh):

time: 100 us -> 87.5 us (0.88)
  local copies, waits for them, and re-layouts: 6.99 us -> 0 us
  Pallas kernels: 92.3 us -> 86.8 us
    pallas_call x1, Pallas kernels: 92.3 us -> 85 us  [local(): pl.pallas_call(kernel, name='ptycho', out_shape=(jax.ShapeDtypeStruct(obj...]
    unnamed x13 -> x0, local copies, waits for them, and re-layouts: 6.99 us -> none
    pallas_call x0 -> x1, Pallas kernels: none -> 1.77 us  [local(): pl.pallas_call(hand_over, name='hand_over', out_shape=tuple((jax.ShapeDty...]
where the time goes in v2:
time: 87.5 us; the launch traced here: 87.4 us
  Pallas kernels  86.8 us (99%)
    pallas_call x1, Pallas kernels, local(): pl.pallas_call(kernel, name='ptycho', out_shape=(jax.ShapeDtypeStruct(obj...  85 us
    pallas_call x1, Pallas kernels, local(): pl.pallas_call(hand_over, name='hand_over', out_shape=tuple((jax.ShapeDty...  1.77 us

profile of v2, /device:TPU:1, one launch (start us, length us, event | category | flops | bytes accessed | tf_op | source)
XLA Modules:
  0.0 87.4 jit_solution(13958496001481386317)
XLA Ops:
  0.6 85.0 %ptycho.1 = (f32[1,2,2,128,128]{4,3,2,1,0:T(8,128)}, f32[4,128,128]{2,1,0:T(8,128)}) custom-call(s32[2,4]{1,0:T(2,128)} %bitcast.1, f32[1,2,2,128,128]{4,3,2,1,0:T(8,128)} %obj_in.1, f32[4,2,128,128]{3,2,1,0:T(8,128)} %probe_in.1, f32[128,128]{1,0:T(8,128)} %phase_in.1, f32[4,128,128]{2,1,0:T(8,128)} %meas_in.1, bf16[2,512,256]{2,1,0:T(8,128)(2,1)} %constant.2.clone.table_in), custom_call_target="tpu_custom_call" | custom-call | tf_op jit(solution)/shard_map/ptycho/pallas_call | solution.py:531
  85.7 1.8 %hand_over.1 = (f32[1,2,2,128,128]{4,3,2,1,0:T(8,128)}, f32[4,128,128]{2,1,0:T(8,128)}) custom-call(f32[1,2,2,128,128]{4,3,2,1,0:T(8,128)} %get-tuple-element.4.obj_in, f32[4,128,128]{2,1,0:T(8,128)} %get-tuple-element.5.int_in), custom_call_target="tpu_custom_call" | custom-call | tf_op jit(solution)/shard_map/hand_over/pallas_call | solution.py:545

commit v3 on v2

--- a/solution.py
+++ b/solution.py
@@ -15,6 +15,7 @@
 STEPS = 2
 TILE_COLS = 8
 WAVES = 8
+SEND_ORDER = (0, 3, 1, 2, 4, 5, 6, 7)
 
 MESH = pl.DeviceIdType.MESH
 f32 = jnp.float32
@@ -93,7 +94,7 @@
 
 
 def kernel(
-    pos,
+    pos_in,
     obj_in,
     probe_in,
     phase_in,
@@ -101,6 +102,7 @@
     table_in,
     obj_out,
     int_out,
+    pos,
     table,
     phase,
     probe,
@@ -164,18 +166,19 @@
             device_id=to, device_id_type=MESH,
         )
 
+    barrier = pltpu.get_barrier_semaphore()
+    partners = [up, down, left, right, up_left, up_right, down_left, down_right] + group[1:]
+    for who in partners:
+        pl.semaphore_signal(barrier, inc=1, device_id=who, device_id_type=MESH)
+
     load_plane = pltpu.make_async_copy(obj_in.at[0, core, comp], plane_now, in_sem.at[0])
     load_probe = pltpu.make_async_copy(probe_in, probe.at[pl.ds(0, 4)], in_sem.at[1])
     load_phase = pltpu.make_async_copy(phase_in, phase, in_sem.at[2])
     load_meas = pltpu.make_async_copy(meas_in, meas, in_sem.at[3])
     load_table = pltpu.make_async_copy(table_in, table, in_sem.at[4])
-    for copy in (load_plane, load_probe, load_phase, load_meas, load_table):
+    load_pos = pltpu.make_async_copy(pos_in, pos, in_sem.at[5])
+    for copy in (load_plane, load_pos, load_probe, load_phase, load_meas, load_table):
         copy.start()
-
-    barrier = pltpu.get_barrier_semaphore()
-    partners = [up, down, left, right, up_left, up_right, down_left, down_right] + group[1:]
-    for who in partners:
-        pl.semaphore_signal(barrier, inc=1, device_id=who, device_id_type=MESH)
 
     def row_ok():
         row = lax.broadcasted_iota(jnp.int32, (EXT, K), 0)
@@ -189,11 +192,11 @@
         for i, (block, to) in enumerate(zip(corners, (tl, th, bl, bh))):
             corner_send[e, i] = block
             copies.append(remote(corner_send.at[e, i], corner_recv.at[e, i], s_corner.at[e, i], r_corner.at[e, i], to))
-            copies[-1].start()
         for i, (block, to) in enumerate(zip((top, bottom, side_low, side_high), (up, down, low_side, high_side))):
             edge_send[e, i] = block
             copies.append(remote(edge_send.at[e, i], edge_recv.at[e, i], s_edge.at[e, i], r_edge.at[e, i], to))
-            copies[-1].start()
+        for i in SEND_ORDER:
+            copies[i].start()
         return copies
 
     def arrived(copies):
@@ -312,6 +315,7 @@
     for half in range(2):
         placed[half] = jnp.zeros((384, K), f32)
     load_meas.wait()
+    load_pos.wait()
     load_table.wait()
     take_edges(0, plane_now[...], first_copies)
     win_copies = send_windows(0)
@@ -492,9 +496,11 @@
 
 def local(object_tiles, probe, propagator_phase, measured, positions):
     anywhere = pl.BlockSpec(memory_space=pl.ANY)
+    in_vmem = pl.BlockSpec(memory_space=pltpu.VMEM)
     dma = pltpu.SemaphoreType.DMA
     V = pltpu.VMEM
     scratch = [
+        pltpu.SMEM((2, 4), jnp.int32),
         V((2, 2 * EXT, EXT), bf16),
         V((K, K), f32),
         V((12, 2, K, K), f32),
@@ -517,7 +523,7 @@
         V((4, 4, HALO, K), f32),
         V((4, 4, 32, K), f32),
         V((4, 4, 32, K), f32),
-        dma((5,)),
+        dma((6,)),
         dma((3,)),
         dma((5,)), dma((5,)),
         dma((2, 3)), dma((2, 3)),
@@ -532,11 +538,11 @@
         kernel,
         name="ptycho",
         out_shape=(
-            jax.ShapeDtypeStruct(object_tiles.shape, f32),
-            jax.ShapeDtypeStruct(measured.shape, f32),
+            V(object_tiles.shape, f32),
+            V(measured.shape, f32),
         ),
-        in_specs=[pl.BlockSpec(memory_space=pltpu.SMEM)] + [anywhere] * 5,
-        out_specs=(anywhere, anywhere),
+        in_specs=[anywhere] * 6,
+        out_specs=(in_vmem, in_vmem),
         scratch_shapes=scratch,
         compiler_params=pltpu.CompilerParams(
             collective_id=0, has_side_effects=True
@@ -548,26 +554,20 @@
         out_shape=tuple(jax.ShapeDtypeStruct(x.shape, f32) for x in outs),
         in_specs=[anywhere] * 2,
         out_specs=(anywhere, anywhere),
-        scratch_shapes=[V(x.shape, f32) for x in outs] + [dma((2,)), dma((2,))],
+        scratch_shapes=[dma((2,))],
+        compiler_params=pltpu.CompilerParams(vmem_limit_bytes=1024 * 1024),
     )(*outs)
 
 
-def hand_over(obj_in, int_in, obj_out, int_out, obj, inten, in_sem, out_sem):
-    ins = [
-        pltpu.make_async_copy(obj_in, obj, in_sem.at[0]),
-        pltpu.make_async_copy(int_in, inten, in_sem.at[1]),
+def hand_over(obj, inten, obj_out, int_out, sem):
+    copies = [
+        pltpu.make_async_copy(obj, obj_out, sem.at[0]),
+        pltpu.make_async_copy(inten, int_out, sem.at[1]),
     ]
-    outs = [
-        pltpu.make_async_copy(obj, obj_out, out_sem.at[0]),
-        pltpu.make_async_copy(inten, int_out, out_sem.at[1]),
-    ]
-    for copy in ins:
+    for copy in copies:
         copy.start()
-    for copy, out in zip(ins, outs):
+    for copy in copies:
         copy.wait()
-        out.start()
-    for out in outs:
-        out.wait()
 
 
 def solution(mesh):

time: 87.5 us -> 85.1 us (0.973)
  Pallas kernels: 86.8 us -> 83.9 us
    pallas_call x1, Pallas kernels: 85 us -> 83.1 us  [local(): pl.pallas_call(kernel, name='ptycho', out_shape=(V(object_tiles.shape, f3...]
    pallas_call x1, Pallas kernels: 1.77 us -> 0.81 us  [local(): pl.pallas_call(hand_over, name='hand_over', out_shape=tuple((jax.ShapeDty...]
where the time goes in v3:
time: 85.1 us; the launch traced here: 84.7 us
  Pallas kernels  83.9 us (99%)
    pallas_call x1, Pallas kernels, local(): pl.pallas_call(kernel, name='ptycho', out_shape=(V(object_tiles.shape, f3...  83.1 us

profile of v3, /device:TPU:1, one launch (start us, length us, event | category | flops | bytes accessed | tf_op | source)
XLA Modules:
  0.0 84.7 jit_solution(8313607708861042345)
XLA Ops:
  0.6 83.1 %ptycho.1 = (f32[1,2,2,128,128]{4,3,2,1,0:T(8,128)S(1)}, f32[4,128,128]{2,1,0:T(8,128)S(1)}) custom-call(s32[2,4]{1,0:T(2,128)} %bitcast.1, f32[1,2,2,128,128]{4,3,2,1,0:T(8,128)} %obj_in.1, f32[4,2,128,128]{3,2,1,0:T(8,128)} %probe_in.1, f32[128,128]{1,0:T(8,128)} %phase_in.1, f32[4,128,128]{2,1,0:T(8,128)} %meas_in.1, ...), custom_call_target="tpu_custom_call" | custom-call | tf_op jit(solution)/shard_map/ptycho/pallas_call | solution.py:537
  83.7 0.8 hand_over.1

commit v4 on v3

--- a/solution.py
+++ b/solution.py
@@ -469,8 +469,7 @@
         inner = jnp.where(ok, inner + inner2, 0.0)
         outer = jnp.where(ok, outer + outer2, 0.0)
         keep_int.start()
-        total = fold(1 + 2 * n, inner, outer, probe_copies[3 + n : 4 + n] if n == 0 else [])
-        send_int.start()
+        total = fold(1 + 2 * n, inner, outer, [probe_copies[3], send_int] if n == 0 else [send_int])
         pending += [keep_int, send_int]
         plane_now[...] = plane_now[...] - total
         if n + 1 < STEPS:

time: 85.1 us -> 84.5 us (level)
  no operation moved by 1% of the time
where the time goes in v4:
time: 84.5 us; the launch traced here: 84.3 us
  Pallas kernels  83.5 us (99%)
    pallas_call x1, Pallas kernels, local(): pl.pallas_call(kernel, name='ptycho', out_shape=(V(object_tiles.shape, f3...  82.7 us

profile of v4, /device:TPU:1, one launch (start us, length us, event | category | flops | bytes accessed | tf_op | source)
XLA Modules:
  0.0 84.3 jit_solution(10674254688580119150)
XLA Ops:
  0.6 82.7 %ptycho.1 = (f32[1,2,2,128,128]{4,3,2,1,0:T(8,128)S(1)}, f32[4,128,128]{2,1,0:T(8,128)S(1)}) custom-call(s32[2,4]{1,0:T(2,128)} %bitcast.1, f32[1,2,2,128,128]{4,3,2,1,0:T(8,128)} %obj_in.1, f32[4,2,128,128]{3,2,1,0:T(8,128)} %probe_in.1, f32[128,128]{1,0:T(8,128)} %phase_in.1, f32[4,128,128]{2,1,0:T(8,128)} %meas_in.1, ...), custom_call_target="tpu_custom_call" | custom-call | tf_op jit(solution)/shard_map/ptycho/pallas_call | solution.py:536
  83.3 0.8 hand_over.1
